TPU v7x, 128 devices: a whole 4x4x4 slice. The times are simulated.
128 devices in a mesh: dp: 8 (over x, core), fsdp: 16 (over z, y).
Axes of the slice: x: 4, y: 4, z: 4, core: 2. Of those that a mesh axis runs over, the one named last changes fastest.
Arguments:
- tokens: bfloat16 [65536, 1408], P(('dp', 'fsdp')), may hold values from -6 to 6
- image_of: int32 [65536], P(('dp', 'fsdp')), may hold values from 0 to 16383, as said below
- live: int32 [65536], P(('dp', 'fsdp')), may hold values from 0 to 1, as said below
- request_of: int32 [16384], P('dp'), may hold values from -1 to 63, as said below
- ln1_gain: float32 [1408], replicated, may hold values from 0.5 to 1.5
- ln1_shift: float32 [1408], replicated, may hold values from -3 to 3
- w_qkv: bfloat16 [1408, 4224], P('fsdp')
- b_qkv: float32 [4224], replicated, may hold values from -3 to 3
- w_out: bfloat16 [1408, 1408], P('fsdp'), may hold values from -0.15625 to 0.15625
- b_out: float32 [1408], replicated, may hold values from -3 to 3
- ln2_gain: float32 [1408], replicated, may hold values from 0.5 to 1.5
- ln2_shift: float32 [1408], replicated, may hold values from -3 to 3
- w_proj: bfloat16 [5632, 4096], P(None, 'fsdp'), may hold values from -0.078125 to 0.078125
- b_proj: float32 [4096], P('fsdp'), may hold values from -3 to 3
Outputs:
- features: bfloat16 [16384, 4096], P('dp', 'fsdp')
- peaks: float32 [64], replicated
Inputs may be any that keep to these rules, and one draw needn't show every extreme that they name: `image_of`: tokens come in aligned groups of 4 of one image; an image's tokens are consecutive and lie within one aligned block of 512 rows; numbers never fall along the rows; the last block's last group of 4 is an image of its own. Padding fills whole groups of 4 at the end of each aligned block of 512 rows, at most half of the block; the first group of every block is live and the last block has none; a padding token carries the image number of the token before it. `request_of`: -1 exactly on merged rows of padding; on the other rows request numbers never fall along the rows, and every request has some row.
All inputs are finite; a program needn't handle non-finite values.
Results may differ from a plain program's by a relative error of at most 0.012.
The roundings to bfloat16 on the way count: a program that leaves them out, or rounds other values in their place, can miss the bound.
Values may be sent and summed in bfloat16 or wider, within the bound.
A program may use at most 192 MiB of HBM per device.

v0:
```python
import jax
import jax.numpy as jnp
from jax import lax
from jax.sharding import PartitionSpec as P

HEADS = 16


def normalize(values, gain, shift):
    mean_value = jnp.mean(values, axis=-1, keepdims=True)
    centred = values - mean_value
    variance = jnp.mean(centred * centred, axis=-1, keepdims=True)
    return centred * lax.rsqrt(variance + 1e-06) * gain + shift


def attention(qkv, image_ids, live_flags, heads):
    count_rows = qkv.shape[0]
    width = qkv.shape[1] // 3
    head_size = width // heads
    scale = head_size ** (-0.5)
    queries = qkv[:, :width].reshape(count_rows, heads, head_size)
    keys_all = qkv[:, width : 2 * width].reshape(count_rows, heads, head_size)
    values_all = qkv[:, 2 * width :].reshape(count_rows, heads, head_size)
    block_rows = min(512, count_rows)
    blocks = count_rows // block_rows
    key_live = live_flags[None, :] == 1

    def one_block(items):
        block_queries, block_images = items
        scores = (
            jnp.einsum("qhe,khe->hqk", block_queries, keys_all, preferred_element_type=jnp.float32)
            * scale
        )
        allowed = (block_images[:, None] == image_ids[None, :]) & key_live
        scores = jnp.where(allowed[None], scores, jnp.float32(-1e30))
        top = jnp.max(scores, axis=-1, keepdims=True)
        expo = jnp.exp(scores - top)
        weights = (expo / jnp.sum(expo, axis=-1, keepdims=True)).astype(jnp.bfloat16)
        mixed = jnp.einsum("hqk,khe->qhe", weights, values_all, preferred_element_type=jnp.float32)
        return mixed.reshape(block_rows, width).astype(jnp.bfloat16)

    result = lax.map(
        one_block,
        (
            queries.reshape(blocks, block_rows, heads, head_size),
            image_ids.reshape(blocks, block_rows),
        ),
    )
    return result.reshape(count_rows, width)


def shards(
    tokens,
    image_of,
    live,
    request_of,
    ln1_gain,
    ln1_shift,
    w_qkv,
    b_qkv,
    w_out,
    b_out,
    ln2_gain,
    ln2_shift,
    w_proj,
    b_proj,
):
    count_rows = tokens.shape[0]
    width = tokens.shape[1]
    resid = tokens.astype(jnp.float32)
    normed = normalize(resid, ln1_gain, ln1_shift).astype(jnp.bfloat16)
    columns = normed
    mixed = jnp.dot(
        columns,
        lax.all_gather(w_qkv, "fsdp", axis=0, tiled=True),
        preferred_element_type=jnp.float32,
    )
    qkv = (mixed + b_qkv).astype(jnp.bfloat16)
    attended = attention(qkv, image_of, live, HEADS)
    columns = attended
    projected_out = jnp.dot(
        columns,
        lax.all_gather(w_out, "fsdp", axis=0, tiled=True),
        preferred_element_type=jnp.float32,
    )
    resid = resid + (projected_out + b_out)
    normed2 = normalize(resid, ln2_gain, ln2_shift).astype(jnp.bfloat16)
    merged = normed2.reshape(count_rows // 4, 4 * width)
    projected = (
        jnp.dot(
            lax.all_gather(merged, "fsdp", axis=0, tiled=True),
            w_proj,
            preferred_element_type=jnp.float32,
        )
        + b_proj
    )
    requests = lax.axis_size("dp") * lax.axis_size("fsdp") // 2
    columns_here = projected.shape[1]
    labels = jnp.arange(requests, dtype=jnp.int32)
    member = request_of[:, None] == labels[None, :]
    row_squares = jnp.sum(projected * projected, axis=1)
    row_top = jnp.max(projected, axis=1)
    sums_part = jnp.sum(jnp.where(member, row_squares[:, None], jnp.float32(0.0)), axis=0)
    entries_part = jnp.sum(member.astype(jnp.float32), axis=0) * jnp.float32(columns_here)
    top_part = jnp.max(jnp.where(member, row_top[:, None], jnp.float32(-jnp.inf)), axis=0)
    sumsq, entries = lax.psum((sums_part, entries_part), ("dp", "fsdp"))
    top = lax.pmax(top_part, ("dp", "fsdp"))
    rms = jnp.sqrt(sumsq / entries + 1e-06)
    valid = request_of >= 0
    row_rms = jnp.sum(jnp.where(member, rms[None, :], jnp.float32(0.0)), axis=1) + jnp.where(
        valid, 0.0, 1.0
    )
    features = jnp.where(valid[:, None], projected / row_rms[:, None], jnp.float32(0.0)).astype(
        jnp.bfloat16
    )
    peaks = top / rms
    return (features, peaks)


def solution(mesh):
    return jax.shard_map(
        shards,
        mesh=mesh,
        in_specs=(
            P(("dp", "fsdp"), None),
            P(("dp", "fsdp")),
            P(("dp", "fsdp")),
            P("dp"),
            P(),
            P(),
            P("fsdp", None),
            P(),
            P("fsdp", None),
            P(),
            P(),
            P(),
            P(None, "fsdp"),
            P("fsdp"),
        ),
        out_specs=(P("dp", "fsdp"), P()),
        check_vma=False,
    )
```

profile of v0, /device:TPU:1, one launch (start us, length us, event | category | flops | bytes accessed | tf_op | source)
XLA Modules:
  0.0 461.9 jit_solution(2938531197813447947)
XLA Ops:
  7.2 0.0 all-gather.4.cloned.1.call-start
  7.3 0.7 all-gather.4.cloned.1.call-update
  8.0 0.0 all-gather.6.cloned.1.call-start
  8.0 0.7 all-gather.6.cloned.1.call-update
  8.7 0.0 all-gather.8.cloned.1.call-start
  8.8 1.6 convert_reduce_fusion
  10.4 1.9 fusion.8
  12.3 0.2 compare_and_fusion
  12.6 87.9 %all-gather.4.cloned.1.call-done = bf16[1408,4224]{1,0:T(8,128)(2,1)} async-done(((bf16[88,4224]{1,0:T(8,128)(2,1)}), bf16[1408,4224]{1,0:T(8,128)(2,1)}) %all-gather.4.cloned.1.call-update) | async-done | bytes 11894800 | tf_op jit(solution)/shard_map/all_gather | solution.py:75
  100.5 12.4 %add_convert_fusion = bf16[512,4224]{1,0:T(8,128)(2,1)S(1)} fusion(bf16[1408,4224]{1,0:T(8,128)(2,1)} %all-gather.4.cloned.1.call-done, f32[4224]{0:T(1024)S(1)} %copy-done.7, bf16[512,1408]{1,0:T(8,128)(2,1)} %param.14, f32[1408]{0:T(1024)S(1)} %copy-done.8, f32[1408]{0:T(1024)S(1)} %copy-done.9, f32[512]{0:T(512)S(1)} %add_rsqrt_fusion.1, ...), kind=kOutput, calls=%fused_computation.5 | convolution fusion | flops 6098780160 | bytes 17694208 | tf_op jit(solution)/shard_map/dot_general | solution.py:73
  112.8 2.1 fusion.23
  115.0 2.6 copy.27
  117.6 2.5 copy.28
  120.1 2.6 copy.26
  122.7 11.0 %fusion.24 = (f32[16,512]{1,0:T(8,128)S(1)}, f32[16,512,512]{1,2,0:T(8,128)}) fusion(pred[512,512]{0,1:T(8,128)(4,1)S(1)} %compare_and_fusion, bf16[512,16,88]{0,2,1:T(8,128)(2,1)} %bitcast.17, bf16[512,16,88]{0,2,1:T(8,128)(2,1)} %bitcast.18), kind=kOutput, calls=%fused_computation.50 | convolution fusion | flops 754975232 | bytes 19955712 | tf_op jit(solution)/shard_map/while/body/eval_jaxpr/sub | solution.py:37
  133.7 8.9 %fusion.14 = bf16[16,88,512]{2,1,0:T(8,128)(2,1)} fusion(bf16[512,16,88]{0,2,1:T(8,128)(2,1)} %bitcast.19, f32[16,512,512]{1,2,0:T(8,128)} %get-tuple-element.46, f32[16,512]{1,0:T(8,128)S(1)} %get-tuple-element.45), kind=kOutput, calls=%fused_computation.26 | convolution fusion | flops 747307008 | bytes 19693568 | tf_op jit(solution)/shard_map/while/body/eval_jaxpr/hqk,khe->qhe/dot_general | solution.py:39
  142.5 10.3 %all-gather.6.cloned.1.call-done = bf16[1408,1408]{1,0:T(8,128)(2,1)} async-done(((bf16[88,1408]{1,0:T(8,128)(2,1)}), bf16[1408,1408]{1,0:T(8,128)(2,1)}) %all-gather.6.cloned.1.call-update) | async-done | bytes 3964944 | tf_op jit(solution)/shard_map/all_gather | solution.py:83
  152.9 5.9 %fusion.25 = (f32[512]{0:T(512)S(1)}, f32[512,1408]{1,0:T(8,128)S(1)}) fusion(f32[1408]{0:T(1024)S(1)} %copy-done.2, bf16[512,1408]{0,1:T(8,128)(2,1)} %bitcast.16, bf16[1408,1408]{1,0:T(8,128)(2,1)} %all-gather.6.cloned.1.call-done, bf16[512,1408]{1,0:T(8,128)(2,1)} %param.14), kind=kOutput, calls=%fused_computation.51 | convolution fusion | flops 2032926208 | bytes 9739776 | tf_op jit(solution)/shard_map/dot_general | solution.py:81
  158.8 0.4 multiply_reduce_fusion
  159.3 0.2 copy-done.3
  159.5 1.7 add_convert_fusion.1
  161.2 3.6 reshape.109
  164.8 0.0 all-gather.8.cloned.1.call-update
  164.8 143.3 %all-gather.8.cloned.1.call-done = bf16[2048,5632]{1,0:T(8,128)(2,1)} async-done(((bf16[128,5632]{1,0:T(8,128)(2,1)}), bf16[2048,5632]{1,0:T(8,128)(2,1)}) %all-gather.8.cloned.1.call-update) | async-done | bytes 23068688 | tf_op jit(solution)/shard_map/all_gather | solution.py:91
  308.2 12.5 %fusion.22 = (f32[2048]{0:T(1024)S(1)}, f32[2048]{0:T(1024)S(1)}, f32[2048,256]{0,1:T(8,128)}) fusion(f32[256]{0:T(256)S(1)} %copy-done.10, bf16[2048,5632]{1,0:T(8,128)(2,1)} %all-gather.8.cloned.1.call-done, bf16[5632,256]{1,0:T(8,128)(2,1)S(1)} %copy-done), kind=kOutput, calls=%fused_computation.48 | convolution fusion | flops 5907673088 | bytes 28066816 | tf_op jit(solution)/shard_map/dot_general | solution.py:90
  320.7 0.2 convert_reduce_fusion.1
  320.9 64.6 %all-reduce = (f32[64]{0:T(128)S(1)}, f32[64]{0:T(128)S(1)}) all-reduce(f32[64]{0:T(128)S(1)} %get-tuple-element.37, f32[64]{0:T(128)S(1)} %broadcast_multiply_fusion.2), channel_id=1, replica_groups=mesh['dp'=8,'fsdp'=16] {'dp','fsdp'}, use_global_device_ids=true, to_apply=%region_8.9 | all-reduce | flops 128 | bytes 1024 | tf_op jit(solution)/shard_map/psum | solution.py:106
  385.5 0.2 select_reduce_fusion
  385.7 64.1 %pmax.7 = f32[64]{0:T(128)S(1)} all-reduce(f32[64]{0:T(128)S(1)} %get-tuple-element.34), channel_id=1, replica_groups=mesh['dp'=8,'fsdp'=16] {'dp','fsdp'}, use_global_device_ids=true, to_apply=%region_14.15 | all-reduce | flops 64 | bytes 512 | tf_op jit(solution)/shard_map/pmax | solution.py:107
  449.8 0.5 div.47
  450.3 2.8 select_convert_fusion
  453.2 2.3 copy.30
  (29 shorter events, 0.1 us)
Async XLA Ops:
  7.2 301.0 %copy-start = (bf16[5632,256]{1,0:T(8,128)(2,1)S(1)}, bf16[5632,256]{1,0:T(8,128)(2,1)}, u32[]{:S(2)}) copy-start(bf16[5632,256]{1,0:T(8,128)(2,1)} %param.26) | copy-start | bytes 8650756
  7.2 5.1 %copy-start.6 = (s32[512]{0:T(512)S(1)}, s32[512]{0:T(512)}, u32[]{:S(2)}) copy-start(s32[512]{0:T(512)} %param.16) | copy-start | bytes 6148
  7.2 5.1 %copy-start.5 = (s32[512]{0:T(512)S(1)}, s32[512]{0:T(512)}, u32[]{:S(2)}) copy-start(s32[512]{0:T(512)} %param.15) | copy-start | bytes 6148
  7.2 93.3 %copy-start.9 = (f32[1408]{0:T(1024)S(1)}, f32[1408]{0:T(1024)}, u32[]{:S(2)}) copy-start(f32[1408]{0:T(1024)} %param.18) | copy-start | bytes 16900
  7.2 93.3 %copy-start.8 = (f32[1408]{0:T(1024)S(1)}, f32[1408]{0:T(1024)}, u32[]{:S(2)}) copy-start(f32[1408]{0:T(1024)} %param.19) | copy-start | bytes 16900
  7.2 93.3 %copy-start.7 = (f32[4224]{0:T(1024)S(1)}, f32[4224]{0:T(1024)}, u32[]{:S(2)}) copy-start(f32[4224]{0:T(1024)} %param.21) | copy-start | bytes 50692
  7.2 93.2 %all-gather.4.cloned.1.call-start = ((), (), s32[]{:S(2)}) async-start(), calls=%async_computation | async-start | bytes 12638208 | tf_op jit(solution)/shard_map/all_gather | solution.py:75
  8.0 144.9 %all-gather.6.cloned.1.call-start = ((), (), s32[]{:S(2)}) async-start(), calls=%async_computation.1 | async-start | bytes 4212736 | tf_op jit(solution)/shard_map/all_gather | solution.py:83
  8.7 299.4 %all-gather.8.cloned.1.call-start = ((), (), s32[]{:S(2)}) async-start(), calls=%async_computation.2 | async-start | bytes 24510464 | tf_op jit(solution)/shard_map/all_gather | solution.py:91
  133.7 19.2 %copy-start.2 = (f32[1408]{0:T(1024)S(1)}, f32[1408]{0:T(1024)}, u32[]{:S(2)}) copy-start(f32[1408]{0:T(1024)} %param.23) | copy-start | bytes 16900
  158.8 0.7 copy-start.3
  158.8 0.7 copy-start.4
  161.2 147.0 %copy-start.10 = (f32[256]{0:T(256)S(1)}, f32[256]{0:T(256)}, u32[]{:S(2)}) copy-start(f32[256]{0:T(256)} %param.27) | copy-start | bytes 3076
  164.8 155.8 %copy-start.1 = (s32[2048]{0:T(1024)S(1)}, s32[2048]{0:T(1024)}, u32[]{:S(2)}) copy-start(s32[2048]{0:T(1024)} %param.17) | copy-start | bytes 24580
Sparse Core Ops, SparseCore 0:
  10.2 90.2 all-gather.3
  102.6 50.2 all-gather.5
  164.9 143.1 all-gather.7
where the time goes:
time: 462 us
  waiting for transfers between devices  243 us (53%)
  blocking collectives  129 us (28%)
  matrix products  50.6 us (11%)
  local copies, waits for them, and re-layouts  16 us (3%)
  between operations  13.9 us (3%)
  other arithmetic  9.62 us (2%)
    all_gather x1, waiting for transfers between devices, shards(): lax.all_gather(merged, 'fsdp', axis=0, tiled=True)  143 us
    all_gather x1, waiting for transfers between devices, shards(): lax.all_gather(w_qkv, 'fsdp', axis=0, tiled=True)  87.9 us
    psum x1, blocking collectives, shards(): sumsq, entries = lax.psum((sums_part, entries_part), ('dp', 'fsdp'))  64.6 us
    pmax x1, blocking collectives, shards(): top = lax.pmax(top_part, ('dp', 'fsdp'))  64.1 us
    dot_general x1, matrix products, shards(): jnp.dot(lax.all_gather(merged, 'fsdp', axis=0, tiled=True), w_proj, prefe...  12.5 us
    dot_general x1, matrix products, shards(): jnp.dot(columns, lax.all_gather(w_qkv, 'fsdp', axis=0, tiled=True), prefe...  12.4 us
    sub x1, matrix products, one_block(): expo = jnp.exp(scores - top)  11 us
    all_gather x1, waiting for transfers between devices, shards(): lax.all_gather(w_out, 'fsdp', axis=0, tiled=True)  10.3 us
  transfers between devices with their start and end apart: 3, of which 3 were waited for; matrix products, arithmetic and copies ran while one was open for 10% of the time, Pallas kernels for 0%

commit v1 on v0

--- a/solution.py
+++ b/solution.py
@@ -88,7 +88,10 @@
     merged = normed2.reshape(count_rows // 4, 4 * width)
     projected = (
         jnp.dot(
-            lax.all_gather(merged, "fsdp", axis=0, tiled=True),
+            jnp.concatenate(
+                lax.all_to_all(jnp.stack(lax.axis_size("fsdp") * [merged], axis=0), "fsdp", 0, 0),
+                axis=0,
+            ),
             w_proj,
             preferred_element_type=jnp.float32,
         )

time: 462 us -> 581 us (1.26)
  blocking collectives: 129 us -> 385 us
  waiting for transfers between devices: 243 us -> 99.7 us
    all_to_all x0 -> x1, blocking collectives: none -> 257 us  [shards(): lax.all_to_all(jnp.stack(lax.axis_size('fsdp') * [merged], axis=0), 'fsdp...]
    all_gather x1 -> x0, waiting for transfers between devices: 143 us -> none  [shards(): lax.all_gather(merged, 'fsdp', axis=0, tiled=True)]
    another operation x0 -> x2, local copies, waits for them, and re-layouts: none -> 8.36 us  [shards(): jnp.stack(lax.axis_size('fsdp') * [merged], axis=0)]
  transfers between devices with their start and end apart: 3 -> 2, of which waited for: 3 -> 2; matrix products, arithmetic and copies ran while one was open for 10% -> 8% of each run, Pallas kernels for 0% -> 0%
where the time goes in v1:
time: 581 us; the launch traced here: 580 us
  blocking collectives  385 us (66%)
  waiting for transfers between devices  99.7 us (17%)
  matrix products  50.7 us (9%)
  local copies, waits for them, and re-layouts  20.8 us (4%)
  between operations  14.2 us (2%)
  other arithmetic  9.62 us (2%)
    all_to_all x1, blocking collectives, shards(): lax.all_to_all(jnp.stack(lax.axis_size('fsdp') * [merged], axis=0), 'fsdp...  257 us
    all_gather x1, waiting for transfers between devices, shards(): lax.all_gather(w_qkv, 'fsdp', axis=0, tiled=True)  88 us
    psum x1, blocking collectives, shards(): sumsq, entries = lax.psum((sums_part, entries_part), ('dp', 'fsdp'))  64.2 us
    pmax x1, blocking collectives, shards(): top = lax.pmax(top_part, ('dp', 'fsdp'))  63.8 us
    dot_general x1, matrix products, shards(): jnp.dot(jnp.concatenate(lax.all_to_all(jnp.stack(lax.axis_size('fsdp') *...  12.5 us
    dot_general x1, matrix products, shards(): jnp.dot(columns, lax.all_gather(w_qkv, 'fsdp', axis=0, tiled=True), prefe...  12.4 us
  transfers between devices with their start and end apart: 2, of which 2 were waited for; matrix products, arithmetic and copies ran while one was open for 8% of the time, Pallas kernels for 0%

profile of v1, /device:TPU:1, one launch (start us, length us, event | category | flops | bytes accessed | tf_op | source)
XLA Modules:
  0.0 579.9 jit_solution(2521560944470038648)
XLA Ops:
  7.2 0.0 all-gather.3.cloned.1.call-start
  7.3 0.7 all-gather.3.cloned.1.call-update
  8.0 0.0 all-gather.5.cloned.1.call-start
  8.0 0.7 all-gather.5.cloned.1.call-update
  8.7 1.6 convert_reduce_fusion
  10.3 1.9 fusion.8
  12.3 0.2 compare_and_fusion
  12.5 88.0 %all-gather.3.cloned.1.call-done = bf16[1408,4224]{1,0:T(8,128)(2,1)} async-done(((bf16[88,4224]{1,0:T(8,128)(2,1)}), bf16[1408,4224]{1,0:T(8,128)(2,1)}) %all-gather.3.cloned.1.call-update) | async-done | bytes 11894800 | tf_op jit(solution)/shard_map/all_gather | solution.py:75
  100.5 12.4 %add_convert_fusion = bf16[512,4224]{1,0:T(8,128)(2,1)S(1)} fusion(bf16[1408,4224]{1,0:T(8,128)(2,1)} %all-gather.3.cloned.1.call-done, f32[4224]{0:T(1024)S(1)} %copy-done.7, bf16[512,1408]{1,0:T(8,128)(2,1)} %param.14, f32[1408]{0:T(1024)S(1)} %copy-done.8, f32[1408]{0:T(1024)S(1)} %copy-done.9, f32[512]{0:T(512)S(1)} %add_rsqrt_fusion.1, ...), kind=kOutput, calls=%fused_computation.5 | convolution fusion | flops 6098780160 | bytes 17694208 | tf_op jit(solution)/shard_map/dot_general | solution.py:73
  112.8 2.2 fusion.23
  115.0 2.6 copy.28
  117.6 2.5 copy.27
  120.1 2.6 copy.26
  122.7 11.0 %fusion.24 = (f32[16,512]{1,0:T(8,128)S(1)}, f32[16,512,512]{1,2,0:T(8,128)}) fusion(pred[512,512]{0,1:T(8,128)(4,1)S(1)} %compare_and_fusion, bf16[512,16,88]{0,2,1:T(8,128)(2,1)} %bitcast.20, bf16[512,16,88]{0,2,1:T(8,128)(2,1)} %bitcast.19), kind=kOutput, calls=%fused_computation.50 | convolution fusion | flops 754975232 | bytes 19955712 | tf_op jit(solution)/shard_map/while/body/eval_jaxpr/sub | solution.py:37
  133.7 8.9 %fusion.14 = bf16[16,88,512]{2,1,0:T(8,128)(2,1)} fusion(bf16[512,16,88]{0,2,1:T(8,128)(2,1)} %bitcast.21, f32[16,512,512]{1,2,0:T(8,128)} %get-tuple-element.46, f32[16,512]{1,0:T(8,128)S(1)} %get-tuple-element.45), kind=kOutput, calls=%fused_computation.26 | convolution fusion | flops 747307008 | bytes 19693568 | tf_op jit(solution)/shard_map/while/body/eval_jaxpr/hqk,khe->qhe/dot_general | solution.py:39
  142.6 10.3 %all-gather.5.cloned.1.call-done = bf16[1408,1408]{1,0:T(8,128)(2,1)} async-done(((bf16[88,1408]{1,0:T(8,128)(2,1)}), bf16[1408,1408]{1,0:T(8,128)(2,1)}) %all-gather.5.cloned.1.call-update) | async-done | bytes 3964944 | tf_op jit(solution)/shard_map/all_gather | solution.py:83
  152.9 5.9 %fusion.25 = (f32[512]{0:T(512)S(1)}, f32[512,1408]{1,0:T(8,128)S(1)}) fusion(f32[1408]{0:T(1024)S(1)} %copy-done.2, bf16[512,1408]{0,1:T(8,128)(2,1)} %bitcast.18, bf16[1408,1408]{1,0:T(8,128)(2,1)} %all-gather.5.cloned.1.call-done, bf16[512,1408]{1,0:T(8,128)(2,1)} %param.14), kind=kOutput, calls=%fused_computation.51 | convolution fusion | flops 2032926208 | bytes 9739776 | tf_op jit(solution)/shard_map/dot_general | solution.py:81
  158.8 0.4 multiply_reduce_fusion
  159.3 0.2 copy-done.3
  159.5 0.0 copy-done.4
  159.5 1.7 add_convert_fusion.1
  161.2 3.6 stack_reshape.2
  164.8 4.8 stack.3
  169.6 257.0 %all_to_all.5 = bf16[16,128,5632]{2,1,0:T(8,128)(2,1)} all-to-all(bf16[16,128,5632]{2,1,0:T(8,128)(2,1)S(1)} %stack.3), channel_id=1, replica_groups=mesh['dp'=8,'fsdp'=16] {'fsdp'}, dimensions={0} | all-to-all | bytes 46137344 | tf_op jit(solution)/shard_map/all_to_all | solution.py:92
  426.6 12.5 %fusion.22 = (f32[2048]{0:T(1024)S(1)}, f32[2048]{0:T(1024)S(1)}, f32[2048,256]{0,1:T(8,128)}) fusion(f32[256]{0:T(256)S(1)} %copy-done.10, bf16[2048,5632]{1,0:T(8,128)(2,1)} %bitcast.17, bf16[5632,256]{1,0:T(8,128)(2,1)S(1)} %copy-done), kind=kOutput, calls=%fused_computation.48 | convolution fusion | flops 5907673088 | bytes 28066816 | tf_op jit(solution)/shard_map/dot_general | solution.py:90
  439.1 0.2 convert_reduce_fusion.1
  439.3 64.2 %all-reduce = (f32[64]{0:T(128)S(1)}, f32[64]{0:T(128)S(1)}) all-reduce(f32[64]{0:T(128)S(1)} %get-tuple-element.37, f32[64]{0:T(128)S(1)} %broadcast_multiply_fusion.2), channel_id=1, replica_groups=mesh['dp'=8,'fsdp'=16] {'dp','fsdp'}, use_global_device_ids=true, to_apply=%region_8.9 | all-reduce | flops 128 | bytes 1024 | tf_op jit(solution)/shard_map/psum | solution.py:109
  503.5 0.2 select_reduce_fusion
  503.7 63.8 %pmax.7 = f32[64]{0:T(128)S(1)} all-reduce(f32[64]{0:T(128)S(1)} %get-tuple-element.34), channel_id=1, replica_groups=mesh['dp'=8,'fsdp'=16] {'dp','fsdp'}, use_global_device_ids=true, to_apply=%region_14.15 | all-reduce | flops 64 | bytes 512 | tf_op jit(solution)/shard_map/pmax | solution.py:110
  567.5 0.5 div.47
  568.0 2.8 select_convert_fusion
  570.8 2.3 copy.30
  (28 shorter events, 0.1 us)
Async XLA Ops:
  7.2 419.4 %copy-start = (bf16[5632,256]{1,0:T(8,128)(2,1)S(1)}, bf16[5632,256]{1,0:T(8,128)(2,1)}, u32[]{:S(2)}) copy-start(bf16[5632,256]{1,0:T(8,128)(2,1)} %param.26) | copy-start | bytes 8650756
  7.2 5.0 copy-start.6
  7.2 5.1 copy-start.5
  7.2 93.3 %copy-start.7 = (f32[4224]{0:T(1024)S(1)}, f32[4224]{0:T(1024)}, u32[]{:S(2)}) copy-start(f32[4224]{0:T(1024)} %param.21) | copy-start | bytes 50692
  7.2 93.3 %copy-start.8 = (f32[1408]{0:T(1024)S(1)}, f32[1408]{0:T(1024)}, u32[]{:S(2)}) copy-start(f32[1408]{0:T(1024)} %param.19) | copy-start | bytes 16900
  7.2 93.3 %copy-start.9 = (f32[1408]{0:T(1024)S(1)}, f32[1408]{0:T(1024)}, u32[]{:S(2)}) copy-start(f32[1408]{0:T(1024)} %param.18) | copy-start | bytes 16900
  7.2 93.2 %all-gather.3.cloned.1.call-start = ((), (), s32[]{:S(2)}) async-start(), calls=%async_computation.1 | async-start | bytes 12638208 | tf_op jit(solution)/shard_map/all_gather | solution.py:75
  8.0 144.9 %all-gather.5.cloned.1.call-start = ((), (), s32[]{:S(2)}) async-start(), calls=%async_computation.2 | async-start | bytes 4212736 | tf_op jit(solution)/shard_map/all_gather | solution.py:83
  133.7 19.2 %copy-start.2 = (f32[1408]{0:T(1024)S(1)}, f32[1408]{0:T(1024)}, u32[]{:S(2)}) copy-start(f32[1408]{0:T(1024)} %param.23) | copy-start | bytes 16900
  158.8 0.7 copy-start.3
  158.8 0.7 copy-start.4
  169.6 257.0 %copy-start.10 = (f32[256]{0:T(256)S(1)}, f32[256]{0:T(256)}, u32[]{:S(2)}) copy-start(f32[256]{0:T(256)} %param.27) | copy-start | bytes 3076
  426.6 12.5 %copy-start.1 = (s32[2048]{0:T(1024)S(1)}, s32[2048]{0:T(1024)}, u32[]{:S(2)}) copy-start(s32[2048]{0:T(1024)} %param.17) | copy-start | bytes 24580
Sparse Core Ops, SparseCore 0:
  10.2 90.2 all-gather.2
  102.6 50.2 all-gather.4
